TPU v7x, 32 devices: a whole 2x2x4 slice. The times are simulated.
32 devices in a mesh: gx: 4 (over z), gy: 8 (over y, x, core).
Axes of the slice: x: 2, y: 2, z: 4, core: 2. Of those that a mesh axis runs over, the one named last changes fastest.
Arguments:
- features: bfloat16 [256, 20480], P(None, ('gx', 'gy')), may hold values from 0 to 1.5
- w_first: bfloat16 [20480, 256], P(('gx', 'gy')), may hold values from -0.078125 to 0.078125
- w_label: bfloat16 [256, 90112], P(None, ('gx', 'gy')), may hold values from -42 to 42
- label_ids: int32 [256, 8], replicated, may hold values from 0 to 90111, as said below
- label_count: int32 [256], replicated, may hold values from 1 to 8
Outputs:
- grad_first: bfloat16 [20480, 256], P(('gx', 'gy'))
- grad_label: bfloat16 [256, 90112], P(None, ('gx', 'gy'))
- mean_loss: float32 [], replicated
Inputs may be any that keep to these rules, and one draw needn't show every extreme that they name: `label_ids`: each document's 8 ids are distinct labels; slots at or past label_count are filled with ids that are ignored.
All inputs are finite; a program needn't handle non-finite values.
Results may differ from a plain program's by a relative error of at most 0.0085.
Values may be sent and summed in bfloat16 or wider, within the bound.
No kernel may reach another device: no remote copies, remote signals or barrier semaphores. Data moves between devices by JAX's collectives and lax.ppermute only.
A program may use at most 64 MiB of HBM per device.

v0:
```python
import jax
import jax.numpy as jnp
from jax import lax
from jax.sharding import PartitionSpec as P


def per_device(features, w_first, w_label, label_ids, label_count):
    partial_value = jnp.dot(features, w_first, preferred_element_type=jnp.float32)
    minor_share = lax.psum_scatter(partial_value, "gy", scatter_dimension=0, tiled=True)
    shares = lax.psum(minor_share, "gx")
    hidden = lax.all_gather(jnp.tanh(shares).astype(jnp.bfloat16), "gy", axis=0, tiled=True)
    logits = jnp.dot(hidden, w_label, preferred_element_type=jnp.float32)
    label_width = w_label.shape[1]
    offset = lax.axis_index(("gx", "gy")) * label_width
    local_ids = offset + lax.iota(jnp.int32, label_width)
    slot_total = label_ids.shape[1]
    in_count = lax.iota(jnp.int32, slot_total)[None, :] < label_count[:, None]
    matches = jnp.zeros(logits.shape, jnp.float32)
    for slot_index in range(slot_total):
        hit = in_count[:, slot_index : slot_index + 1] & (
            label_ids[:, slot_index : slot_index + 1] == local_ids[None, :]
        )
        matches = matches + jnp.where(hit, 1.0, 0.0)
    positive = jnp.sum(matches * logits, axis=1)
    local_max = jnp.max(logits, axis=1)
    row_max = lax.pmax(local_max, ("gx", "gy"))
    local_sum = jnp.sum(jnp.exp(logits - row_max[:, None]), axis=1)
    norm_sum, picked = lax.psum((local_sum, positive), ("gx", "gy"))
    lse = row_max + jnp.log(norm_sum)
    doc_count = label_count.astype(jnp.float32)
    mean_loss = jnp.mean(lse - picked / doc_count)
    grad_logits = (jnp.exp(logits - lse[:, None]) - matches / doc_count[:, None]).astype(
        jnp.bfloat16
    )
    grad_label = lax.dot_general(
        hidden, grad_logits, (((0,), (0,)), ((), ())), preferred_element_type=jnp.float32
    ).astype(jnp.bfloat16)
    grad_part = lax.dot_general(
        grad_logits, w_label, (((1,), (1,)), ((), ())), preferred_element_type=jnp.float32
    )
    grad_hidden = lax.psum(grad_part, ("gx", "gy"))
    hidden_wide = hidden.astype(jnp.float32)
    grad_inner = (grad_hidden * (1.0 - hidden_wide * hidden_wide)).astype(jnp.bfloat16)
    grad_first = lax.dot_general(
        features, grad_inner, (((0,), (0,)), ((), ())), preferred_element_type=jnp.float32
    ).astype(jnp.bfloat16)
    return (grad_first, grad_label, mean_loss)


def solution(mesh):
    placed = (P(None, ("gx", "gy")), P(("gx", "gy"), None), P(None, ("gx", "gy")), P(), P())
    return jax.shard_map(
        per_device,
        mesh=mesh,
        in_specs=placed,
        out_specs=(P(("gx", "gy"), None), P(None, ("gx", "gy")), P()),
        check_vma=False,
    )
```

profile of v0, /device:TPU:0, one launch (start us, length us, event | category | flops | bytes accessed | tf_op | source)
XLA Modules:
  0.0 310.3 jit_solution(5411630395774496116)
XLA Ops:
  7.2 0.0 copy-start
  7.2 0.0 reduce-scatter.2.cloned.1.call-start
  7.2 2.1 fusion.5
  9.4 0.0 reduce-scatter.2.cloned.1.call-update
  9.4 0.0 all-reduce.3.cloned.1.call-start
  9.5 0.7 iota_compare_fusion
  10.1 0.7 convert_element_type.25
  10.9 1.0 fusion.3
  11.9 36.2 %reduce-scatter.2.cloned.1.call-done = f32[32,256]{1,0:T(8,128)} async-done(((f32[256,256]{1,0:T(8,128)}), f32[32,256]{1,0:T(8,128)}) %reduce-scatter.2.cloned.1.call-update) | async-done | bytes 32784 | tf_op jit(solution)/shard_map/reduce_scatter | solution.py:9
  48.0 19.6 %psum.28 = f32[32,256]{1,0:T(8,128)S(1)} all-reduce(f32[32,256]{1,0:T(8,128)} %reduce-scatter.2.cloned.1.call-done), channel_id=1, replica_groups=mesh['gx'=4,'gy'=8] {'gx'}, use_global_device_ids=true, to_apply=%region_1.0 | all-reduce | flops 8192 | bytes 65536 | tf_op jit(solution)/shard_map/psum | solution.py:10
  67.6 9.2 %all_gather.3 = bf16[256,256]{1,0:T(8,128)(2,1)S(1)} all-gather(bf16[32,256]{1,0:T(8,128)(2,1)S(1)} %tanh_convert_fusion), channel_id=1, replica_groups=mesh['gx'=4,'gy'=8] {'gy'}, dimensions={0}, use_global_device_ids=true | all-gather | bytes 147456 | tf_op jit(solution)/shard_map/all_gather | solution.py:11
  76.8 2.1 fusion.4
  78.9 37.4 %pmax.7 = f32[256]{0:T(256)S(1)} all-reduce(f32[256]{0:T(256)S(1)} %get-tuple-element.31), channel_id=1, replica_groups=mesh['gx'=4,'gy'=8] {'gx','gy'}, use_global_device_ids=true, to_apply=%region_3.4 | all-reduce | flops 256 | bytes 2048 | tf_op jit(solution)/shard_map/pmax | solution.py:26
  116.3 6.8 %multiply_reduce_fusion = (f32[256]{0:T(256)S(1)}, f32[256]{0:T(256)S(1)}) fusion(f32[256,2816]{1,0:T(8,128)} %get-tuple-element.32, s32[256]{0:T(256)S(1)} %bitcast.31, pred[256]{0:T(512)(128)(4,1)S(1)} %get-tuple-element.12, s32[256]{0:T(256)S(1)} %bitcast.33, pred[256]{0:T(512)(128)(4,1)S(1)} %get-tuple-element.13, s32[256]{0:T(256)S(1)} %bitcast.21, ...), kind=kLoop, calls=%fused_computation.1 | loop fusion | flops 25230848 | bytes 2908160 | tf_op jit(solution)/shard_map/reduce_sum | solution.py:24
  123.1 40.8 %all-reduce = (f32[256]{0:T(256)S(1)}, f32[256]{0:T(256)S(1)}) all-reduce(f32[256]{0:T(256)S(1)} %get-tuple-element.10, f32[256]{0:T(256)S(1)} %get-tuple-element.9), channel_id=1, replica_groups=mesh['gx'=4,'gy'=8] {'gx','gy'}, use_global_device_ids=true, to_apply=%region_5.6 | all-reduce | flops 512 | bytes 4096 | tf_op jit(solution)/shard_map/psum | solution.py:28
  164.0 0.6 subtract_reduce_fusion
  164.6 7.5 %subtract_convert_fusion = bf16[256,2816]{1,0:T(8,128)(2,1)S(1)} fusion(f32[256,2816]{1,0:T(8,128)} %get-tuple-element.32, f32[256]{0:T(256)S(1)} %convert_element_type.25, f32[256]{0:T(256)S(1)} %get-tuple-element.22, s32[256]{0:T(256)S(1)} %bitcast.32, pred[256]{0:T(512)(128)(4,1)S(1)} %get-tuple-element.12, s32[256]{0:T(256)S(1)} %bitcast.34, ...), kind=kLoop, calls=%fused_computation.2 | loop fusion | flops 25231360 | bytes 4348928 | tf_op jit(solution)/shard_map/convert_element_type | solution.py:32
  172.1 0.0 copy-start.1
  172.1 1.3 fusion.6
  173.4 0.0 all-reduce.3.cloned.1.call-update
  173.4 1.7 convolution_convert_fusion
  175.8 124.4 %all-reduce.3.cloned.1.call-done = f32[256,256]{1,0:T(8,128)} async-done(((f32[256,256]{1,0:T(8,128)}), f32[256,256]{1,0:T(8,128)}) %all-reduce.3.cloned.1.call-update) | async-done | bytes 262160 | tf_op jit(solution)/shard_map/psum | solution.py:41
  300.2 1.2 fusion
  301.4 0.9 copy.9
  (7 shorter events, 0.1 us)
Async XLA Ops:
  7.2 69.6 %copy-start = (bf16[256,2816]{1,0:T(8,128)(2,1)S(1)}, bf16[256,2816]{1,0:T(8,128)(2,1)}, u32[]{:S(2)}) copy-start(bf16[256,2816]{1,0:T(8,128)(2,1)} %param.7) | copy-start | bytes 4325380
  7.2 40.8 %reduce-scatter.2.cloned.1.call-start = ((), (), s32[]{:S(2)}) async-start(), calls=%async_computation.1 | async-start | bytes 294912 | tf_op jit(solution)/shard_map/reduce_scatter | solution.py:9
  9.4 290.8 %all-reduce.3.cloned.1.call-start = ((), (), s32[]{:S(2)}) async-start(), calls=%async_computation.2 | async-start | bytes 524288 | tf_op jit(solution)/shard_map/psum | solution.py:41
  76.8 87.2 %copy-start.2 = (s32[256]{0:T(256)S(1)}, s32[256]{0:T(256)}, u32[]{:S(2)}) copy-start(s32[256]{0:T(256)} %param.9) | copy-start | bytes 3076
  172.1 128.1 %copy-start.1 = (bf16[256,640]{1,0:T(8,128)(2,1)S(1)}, bf16[256,640]{1,0:T(8,128)(2,1)}, u32[]{:S(2)}) copy-start(bf16[256,640]{1,0:T(8,128)(2,1)} %param.5) | copy-start | bytes 983044
Sparse Core Ops, SparseCore 0:
  11.6 36.3 reduce-scatter.1
  173.5 126.5 all-reduce.2
where the time goes:
time: 311 us; the launch traced here: 310 us
  waiting for transfers between devices  161 us (52%)
  blocking collectives  107 us (34%)
  other arithmetic  16.3 us (5%)
  between operations  15.9 us (5%)
  matrix products  8.48 us (3%)
    psum x1, waiting for transfers between devices, per_device(): grad_hidden = lax.psum(grad_part, ('gx', 'gy'))  124 us
    psum x1, blocking collectives, per_device(): norm_sum, picked = lax.psum((local_sum, positive), ('gx', 'gy'))  40.8 us
    pmax x1, blocking collectives, per_device(): row_max = lax.pmax(local_max, ('gx', 'gy'))  37.4 us
    reduce_scatter x1, waiting for transfers between devices, per_device(): lax.psum_scatter(partial_value, 'gy', scatter_dimension=0, tiled=True)  36.2 us
    psum x1, blocking collectives, per_device(): shares = lax.psum(minor_share, 'gx')  19.6 us
    all_gather x1, blocking collectives, per_device(): lax.all_gather(jnp.tanh(shares).astype(jnp.bfloat16), 'gy', axis=0, tiled...  9.17 us
    convert_element_type x1, other arithmetic, per_device(): (jnp.exp(logits - lse[:, None]) - matches / doc_count[:, None]).astype(jn...  7.53 us
    reduce_sum x1, other arithmetic, per_device(): positive = jnp.sum(matches * logits, axis=1)  6.79 us
  transfers between devices with their start and end apart: 2, of which 2 were waited for; matrix products, arithmetic and copies ran while one was open for 1% of the time, Pallas kernels for 0%

commit v1 on v0

--- a/solution.py
+++ b/solution.py
@@ -2,6 +2,12 @@
 import jax.numpy as jnp
 from jax import lax
 from jax.sharding import PartitionSpec as P
+
+
+def summed_here(array, mesh_axis):
+    terms = lax.all_gather(array, mesh_axis, axis=0, tiled=False)
+    total = terms.sum(axis=0)
+    return total
 
 
 def per_device(features, w_first, w_label, label_ids, label_count):
@@ -38,7 +44,7 @@
     grad_part = lax.dot_general(
         grad_logits, w_label, (((1,), (1,)), ((), ())), preferred_element_type=jnp.float32
     )
-    grad_hidden = lax.psum(grad_part, ("gx", "gy"))
+    grad_hidden = summed_here(grad_part, ("gx", "gy"))
     hidden_wide = hidden.astype(jnp.float32)
     grad_inner = (grad_hidden * (1.0 - hidden_wide * hidden_wide)).astype(jnp.bfloat16)
     grad_first = lax.dot_general(

time: 311 us -> 264 us (0.85)
  waiting for transfers between devices: 161 us -> 111 us
  other arithmetic: 16.3 us -> 20.3 us
    psum x1 -> x0, waiting for transfers between devices: 124 us -> none  [per_device(): grad_hidden = lax.psum(grad_part, ('gx', 'gy'))]
    all_gather x0 -> x1, waiting for transfers between devices: none -> 74.8 us  [summed_here(): terms = lax.all_gather(array, mesh_axis, axis=0, tiled=False)]
    reduce_sum x0 -> x1, other arithmetic: none -> 3.97 us  [summed_here(): total = terms.sum(axis=0)]
  transfers between devices with their start and end apart: 2 -> 2, of which waited for: 2 -> 2; matrix products, arithmetic and copies ran while one was open for 1% -> 2% of each run, Pallas kernels for 0% -> 0%
where the time goes in v1:
time: 264 us
  waiting for transfers between devices  111 us (42%)
  blocking collectives  107 us (41%)
  other arithmetic  20.3 us (8%)
  between operations  15.9 us (6%)
  matrix products  7.55 us (3%)
    all_gather x1, waiting for transfers between devices, summed_here(): terms = lax.all_gather(array, mesh_axis, axis=0, tiled=False)  74.8 us
    psum x1, blocking collectives, per_device(): norm_sum, picked = lax.psum((local_sum, positive), ('gx', 'gy'))  40.8 us
    pmax x1, blocking collectives, per_device(): row_max = lax.pmax(local_max, ('gx', 'gy'))  37.4 us
    reduce_scatter x1, waiting for transfers between devices, per_device(): lax.psum_scatter(partial_value, 'gy', scatter_dimension=0, tiled=True)  36.2 us
    psum x1, blocking collectives, per_device(): shares = lax.psum(minor_share, 'gx')  19.6 us
    all_gather x1, blocking collectives, per_device(): lax.all_gather(jnp.tanh(shares).astype(jnp.bfloat16), 'gy', axis=0, tiled...  9.17 us
    convert_element_type x1, other arithmetic, per_device(): (jnp.exp(logits - lse[:, None]) - matches / doc_count[:, None]).astype(jn...  7.53 us
    reduce_sum x1, other arithmetic, per_device(): positive = jnp.sum(matches * logits, axis=1)  6.79 us
  transfers between devices with their start and end apart: 2, of which 2 were waited for; matrix products, arithmetic and copies ran while one was open for 2% of the time, Pallas kernels for 0%

profile of v1, /device:TPU:0, one launch (start us, length us, event | category | flops | bytes accessed | tf_op | source)
XLA Modules:
  0.0 263.7 jit_solution(5460447911230874729)
XLA Ops:
  7.2 0.0 copy-start
  7.2 0.0 reduce-scatter.2.cloned.1.call-start
  7.2 2.1 fusion.5
  9.4 0.0 reduce-scatter.2.cloned.1.call-update
  9.4 0.0 all-gather.3.cloned.1.call-start
  9.5 0.7 iota_compare_fusion
  10.1 0.7 convert_element_type.25
  10.9 1.0 fusion.3
  11.9 36.2 %reduce-scatter.2.cloned.1.call-done = f32[32,256]{1,0:T(8,128)} async-done(((f32[256,256]{1,0:T(8,128)}), f32[32,256]{1,0:T(8,128)}) %reduce-scatter.2.cloned.1.call-update) | async-done | bytes 32784 | tf_op jit(solution)/shard_map/reduce_scatter | solution.py:15
  48.0 19.6 %psum.21 = f32[32,256]{1,0:T(8,128)S(1)} all-reduce(f32[32,256]{1,0:T(8,128)} %reduce-scatter.2.cloned.1.call-done), channel_id=1, replica_groups=mesh['gx'=4,'gy'=8] {'gx'}, use_global_device_ids=true, to_apply=%region_1.0 | all-reduce | flops 8192 | bytes 65536 | tf_op jit(solution)/shard_map/psum | solution.py:16
  67.6 9.2 %all_gather.9 = bf16[256,256]{1,0:T(8,128)(2,1)S(1)} all-gather(bf16[32,256]{1,0:T(8,128)(2,1)S(1)} %tanh_convert_fusion), channel_id=1, replica_groups=mesh['gx'=4,'gy'=8] {'gy'}, dimensions={0}, use_global_device_ids=true | all-gather | bytes 147456 | tf_op jit(solution)/shard_map/all_gather | solution.py:17
  76.8 2.1 fusion.4
  78.9 37.4 %pmax.7 = f32[256]{0:T(256)S(1)} all-reduce(f32[256]{0:T(256)S(1)} %get-tuple-element.31), channel_id=1, replica_groups=mesh['gx'=4,'gy'=8] {'gx','gy'}, use_global_device_ids=true, to_apply=%region_3.4 | all-reduce | flops 256 | bytes 2048 | tf_op jit(solution)/shard_map/pmax | solution.py:32
  116.3 6.8 %multiply_reduce_fusion = (f32[256]{0:T(256)S(1)}, f32[256]{0:T(256)S(1)}) fusion(f32[256,2816]{1,0:T(8,128)} %get-tuple-element.32, s32[256]{0:T(256)S(1)} %bitcast.33, pred[256]{0:T(512)(128)(4,1)S(1)} %get-tuple-element.12, s32[256]{0:T(256)S(1)} %bitcast.35, pred[256]{0:T(512)(128)(4,1)S(1)} %get-tuple-element.13, s32[256]{0:T(256)S(1)} %bitcast.23, ...), kind=kLoop, calls=%fused_computation.1 | loop fusion | flops 25230848 | bytes 2908160 | tf_op jit(solution)/shard_map/reduce_sum | solution.py:30
  123.1 40.8 %all-reduce = (f32[256]{0:T(256)S(1)}, f32[256]{0:T(256)S(1)}) all-reduce(f32[256]{0:T(256)S(1)} %get-tuple-element.10, f32[256]{0:T(256)S(1)} %get-tuple-element.9), channel_id=1, replica_groups=mesh['gx'=4,'gy'=8] {'gx','gy'}, use_global_device_ids=true, to_apply=%region_5.6 | all-reduce | flops 512 | bytes 4096 | tf_op jit(solution)/shard_map/psum | solution.py:34
  164.0 0.6 subtract_reduce_fusion
  164.6 7.5 %subtract_convert_fusion = bf16[256,2816]{1,0:T(8,128)(2,1)S(1)} fusion(f32[256,2816]{1,0:T(8,128)} %get-tuple-element.32, f32[256]{0:T(256)S(1)} %convert_element_type.25, f32[256]{0:T(256)S(1)} %get-tuple-element.22, s32[256]{0:T(256)S(1)} %bitcast.34, pred[256]{0:T(512)(128)(4,1)S(1)} %get-tuple-element.12, s32[256]{0:T(256)S(1)} %bitcast.36, ...), kind=kLoop, calls=%fused_computation.2 | loop fusion | flops 25231360 | bytes 4348928 | tf_op jit(solution)/shard_map/convert_element_type | solution.py:38
  172.1 1.3 fusion.6
  173.4 0.0 all-gather.3.cloned.1.call-update
  174.1 1.7 convolution_convert_fusion
  175.8 74.8 %all-gather.3.cloned.1.call-done = f32[8192,256]{1,0:T(8,128)} async-done(((f32[256,256]{1,0:T(8,128)}), f32[8192,256]{1,0:T(8,128)}) %all-gather.3.cloned.1.call-update) | async-done | bytes 8388624 | tf_op jit(solution)/shard_map/all_gather | solution.py:8
  250.6 4.0 %reduce_sum.37 = f32[256,256]{1,0:T(8,128)S(1)} reduce(f32[32,256,256]{2,1,0:T(8,128)} %bitcast.20, f32[]{:T(128)} %constant.9.clone.1), dimensions={0}, to_apply=%region_6.7 | reduce | flops 2031616 | bytes 8650756 | tf_op jit(solution)/shard_map/reduce_sum | solution.py:9
  254.5 0.3 fusion
  254.8 0.9 copy.9
  (8 shorter events, 0.1 us)
Async XLA Ops:
  7.2 69.6 %copy-start = (bf16[256,2816]{1,0:T(8,128)(2,1)S(1)}, bf16[256,2816]{1,0:T(8,128)(2,1)}, u32[]{:S(2)}) copy-start(bf16[256,2816]{1,0:T(8,128)(2,1)} %param.7) | copy-start | bytes 4325380
  7.2 40.8 %reduce-scatter.2.cloned.1.call-start = ((), (), s32[]{:S(2)}) async-start(), calls=%async_computation.1 | async-start | bytes 294912 | tf_op jit(solution)/shard_map/reduce_scatter | solution.py:15
  9.4 241.2 %all-gather.3.cloned.1.call-start = ((), (), s32[]{:S(2)}) async-start(), calls=%async_computation.2 | async-start | bytes 8650752 | tf_op jit(solution)/shard_map/all_gather | solution.py:8
  76.8 87.2 %copy-start.2 = (s32[256]{0:T(256)S(1)}, s32[256]{0:T(256)}, u32[]{:S(2)}) copy-start(s32[256]{0:T(256)} %param.9) | copy-start | bytes 3076
  250.6 4.0 %copy-start.1 = (bf16[256,640]{1,0:T(8,128)(2,1)S(1)}, bf16[256,640]{1,0:T(8,128)(2,1)}, u32[]{:S(2)}) copy-start(bf16[256,640]{1,0:T(8,128)(2,1)} %param.5) | copy-start | bytes 983044
Sparse Core Ops, SparseCore 0:
  11.6 36.3 reduce-scatter.1
  173.6 76.9 all-gather.2

commit v2 on v0

--- a/solution.py
+++ b/solution.py
@@ -1,7 +1,17 @@
+import functools
 import jax
 import jax.numpy as jnp
 from jax import lax
 from jax.sharding import PartitionSpec as P
+
+
+def supply_tables_now(inp, shard_axis, row_axis):
+    for k in (shard_axis, row_axis):
+        inp = jax.lax.psum(inp, k)
+    return inp
+
+
+_follow_region = functools.partial(supply_tables_now, shard_axis="gy", row_axis="gx")
 
 
 def per_device(features, w_first, w_label, label_ids, label_count):
@@ -25,7 +35,7 @@
     local_max = jnp.max(logits, axis=1)
     row_max = lax.pmax(local_max, ("gx", "gy"))
     local_sum = jnp.sum(jnp.exp(logits - row_max[:, None]), axis=1)
-    norm_sum, picked = lax.psum((local_sum, positive), ("gx", "gy"))
+    norm_sum, picked = _follow_region((local_sum, positive))
     lse = row_max + jnp.log(norm_sum)
     doc_count = label_count.astype(jnp.float32)
     mean_loss = jnp.mean(lse - picked / doc_count)

time: 311 us -> 291 us (0.936)
  blocking collectives: 107 us -> 89.5 us
    psum x1 -> x2, blocking collectives: 40.8 us -> 23.4 us  [supply_tables_now(): inp = jax.lax.psum(inp, k)]
where the time goes in v2:
time: 291 us; the launch traced here: 290 us
  waiting for transfers between devices  158 us (54%)
  blocking collectives  89.5 us (31%)
  other arithmetic  16.3 us (6%)
  between operations  15.9 us (5%)
  matrix products  8.49 us (3%)
    psum x1, waiting for transfers between devices, per_device(): grad_hidden = lax.psum(grad_part, ('gx', 'gy'))  122 us
    pmax x1, blocking collectives, per_device(): row_max = lax.pmax(local_max, ('gx', 'gy'))  37.4 us
    reduce_scatter x1, waiting for transfers between devices, per_device(): lax.psum_scatter(partial_value, 'gy', scatter_dimension=0, tiled=True)  36.2 us
    psum x2, blocking collectives, supply_tables_now(): inp = jax.lax.psum(inp, k)  23.4 us
    psum x1, blocking collectives, per_device(): shares = lax.psum(minor_share, 'gx')  19.6 us
    all_gather x1, blocking collectives, per_device(): lax.all_gather(jnp.tanh(shares).astype(jnp.bfloat16), 'gy', axis=0, tiled...  9.17 us
    convert_element_type x1, other arithmetic, per_device(): (jnp.exp(logits - lse[:, None]) - matches / doc_count[:, None]).astype(jn...  7.53 us
    reduce_sum x1, other arithmetic, per_device(): positive = jnp.sum(matches * logits, axis=1)  6.79 us
  transfers between devices with their start and end apart: 2, of which 2 were waited for; matrix products, arithmetic and copies ran while one was open for 1% of the time, Pallas kernels for 0%

profile of v2, /device:TPU:0, one launch (start us, length us, event | category | flops | bytes accessed | tf_op | source)
XLA Modules:
  0.0 290.1 jit_solution(493678034055656992)
XLA Ops:
  7.2 0.0 copy-start
  7.2 0.0 reduce-scatter.2.cloned.1.call-start
  7.2 2.1 fusion.5
  9.4 0.0 reduce-scatter.2.cloned.1.call-update
  9.4 0.0 all-reduce.4.cloned.1.call-start
  9.5 0.7 iota_compare_fusion
  10.1 0.7 convert_element_type.25
  10.9 1.0 fusion.3
  11.9 36.2 %reduce-scatter.2.cloned.1.call-done = f32[32,256]{1,0:T(8,128)} async-done(((f32[256,256]{1,0:T(8,128)}), f32[32,256]{1,0:T(8,128)}) %reduce-scatter.2.cloned.1.call-update) | async-done | bytes 32784 | tf_op jit(solution)/shard_map/reduce_scatter | solution.py:19
  48.0 19.6 %psum.42 = f32[32,256]{1,0:T(8,128)S(1)} all-reduce(f32[32,256]{1,0:T(8,128)} %reduce-scatter.2.cloned.1.call-done), channel_id=1, replica_groups=mesh['gx'=4,'gy'=8] {'gx'}, use_global_device_ids=true, to_apply=%region_1.0 | all-reduce | flops 8192 | bytes 65536 | tf_op jit(solution)/shard_map/psum | solution.py:20
  67.6 9.2 %all_gather.3 = bf16[256,256]{1,0:T(8,128)(2,1)S(1)} all-gather(bf16[32,256]{1,0:T(8,128)(2,1)S(1)} %tanh_convert_fusion), channel_id=1, replica_groups=mesh['gx'=4,'gy'=8] {'gy'}, dimensions={0}, use_global_device_ids=true | all-gather | bytes 147456 | tf_op jit(solution)/shard_map/all_gather | solution.py:21
  76.8 2.1 fusion.4
  78.9 37.4 %pmax.7 = f32[256]{0:T(256)S(1)} all-reduce(f32[256]{0:T(256)S(1)} %get-tuple-element.33), channel_id=1, replica_groups=mesh['gx'=4,'gy'=8] {'gx','gy'}, use_global_device_ids=true, to_apply=%region_3.4 | all-reduce | flops 256 | bytes 2048 | tf_op jit(solution)/shard_map/pmax | solution.py:36
  116.3 6.8 %multiply_reduce_fusion = (f32[256]{0:T(256)S(1)}, f32[256]{0:T(256)S(1)}) fusion(f32[256,2816]{1,0:T(8,128)} %get-tuple-element.34, s32[256]{0:T(256)S(1)} %bitcast.31, pred[256]{0:T(512)(128)(4,1)S(1)} %get-tuple-element.12, s32[256]{0:T(256)S(1)} %bitcast.33, pred[256]{0:T(512)(128)(4,1)S(1)} %get-tuple-element.13, s32[256]{0:T(256)S(1)} %bitcast.21, ...), kind=kLoop, calls=%fused_computation.1 | loop fusion | flops 25230848 | bytes 2908160 | tf_op jit(solution)/shard_map/reduce_sum | solution.py:34
  123.1 12.7 %all-reduce = (f32[256]{0:T(256)S(1)}, f32[256]{0:T(256)S(1)}) all-reduce(f32[256]{0:T(256)S(1)} %get-tuple-element.10, f32[256]{0:T(256)S(1)} %get-tuple-element.9), channel_id=1, replica_groups=mesh['gx'=4,'gy'=8] {'gy'}, use_global_device_ids=true, to_apply=%region_5.6 | all-reduce | flops 512 | bytes 4096 | tf_op jit(solution)/shard_map/psum | solution.py:10
  135.8 10.7 %all-reduce.1 = (f32[256]{0:T(256)S(1)}, f32[256]{0:T(256)S(1)}) all-reduce(f32[256]{0:T(256)S(1)} %get-tuple-element.19, f32[256]{0:T(256)S(1)} %get-tuple-element.20), channel_id=1, replica_groups=mesh['gx'=4,'gy'=8] {'gx'}, use_global_device_ids=true, to_apply=%region_6.7 | all-reduce | flops 512 | bytes 4096 | tf_op jit(solution)/shard_map/psum | solution.py:10
  146.5 0.6 subtract_reduce_fusion
  147.1 7.5 %subtract_convert_fusion = bf16[256,2816]{1,0:T(8,128)(2,1)S(1)} fusion(f32[256,2816]{1,0:T(8,128)} %get-tuple-element.34, f32[256]{0:T(256)S(1)} %convert_element_type.25, f32[256]{0:T(256)S(1)} %get-tuple-element.24, s32[256]{0:T(256)S(1)} %bitcast.32, pred[256]{0:T(512)(128)(4,1)S(1)} %get-tuple-element.12, s32[256]{0:T(256)S(1)} %bitcast.34, ...), kind=kLoop, calls=%fused_computation.2 | loop fusion | flops 25231360 | bytes 4348928 | tf_op jit(solution)/shard_map/convert_element_type | solution.py:42
  154.6 1.3 fusion.6
  155.9 0.0 all-reduce.4.cloned.1.call-update
  155.9 1.7 convolution_convert_fusion
  158.3 121.7 %all-reduce.4.cloned.1.call-done = f32[256,256]{1,0:T(8,128)} async-done(((f32[256,256]{1,0:T(8,128)}), f32[256,256]{1,0:T(8,128)}) %all-reduce.4.cloned.1.call-update) | async-done | bytes 262160 | tf_op jit(solution)/shard_map/psum | solution.py:51
  280.0 1.3 fusion
  281.2 0.9 copy.9
  (8 shorter events, 0.1 us)
Async XLA Ops:
  7.2 69.6 %copy-start = (bf16[256,2816]{1,0:T(8,128)(2,1)S(1)}, bf16[256,2816]{1,0:T(8,128)(2,1)}, u32[]{:S(2)}) copy-start(bf16[256,2816]{1,0:T(8,128)(2,1)} %param.7) | copy-start | bytes 4325380
  7.2 40.8 %reduce-scatter.2.cloned.1.call-start = ((), (), s32[]{:S(2)}) async-start(), calls=%async_computation.1 | async-start | bytes 294912 | tf_op jit(solution)/shard_map/reduce_scatter | solution.py:19
  9.4 270.6 %all-reduce.4.cloned.1.call-start = ((), (), s32[]{:S(2)}) async-start(), calls=%async_computation.2 | async-start | bytes 524288 | tf_op jit(solution)/shard_map/psum | solution.py:51
  76.8 69.7 %copy-start.2 = (s32[256]{0:T(256)S(1)}, s32[256]{0:T(256)}, u32[]{:S(2)}) copy-start(s32[256]{0:T(256)} %param.9) | copy-start | bytes 3076
  154.6 125.3 %copy-start.1 = (bf16[256,640]{1,0:T(8,128)(2,1)S(1)}, bf16[256,640]{1,0:T(8,128)(2,1)}, u32[]{:S(2)}) copy-start(bf16[256,640]{1,0:T(8,128)(2,1)} %param.5) | copy-start | bytes 983044
Sparse Core Ops, SparseCore 0:
  11.6 36.3 reduce-scatter.1
  156.1 123.8 all-reduce.3
